TPU v7x, 32 devices: a whole 2x2x4 slice. The times are simulated.
32 devices in a mesh: dp: 4 (over y, core), ctx: 4 (over z), tsp: 2 (over x).
Axes of the slice: x: 2, y: 2, z: 4, core: 2. Of those that a mesh axis runs over, the one named last changes fastest.
Arguments:
- grad_out: bfloat16 [4, 1024, 8192], P('dp', 'ctx', 'tsp'), may hold values from -6 to 6
- attn_out: bfloat16 [4, 1024, 4096], P('dp', None, 'ctx'), may hold values from -6 to 6
- out_weight: bfloat16 [4096, 8192], P('ctx', 'tsp'), may hold values from -0.0625 to 0.0625
- query: bfloat16 [4, 1024, 4096], P('dp', 'tsp', 'ctx'), may hold values from -128 to 128
- keys: bfloat16 [4, 1024, 512], P('dp'), may hold values from -128 to 128
- values: bfloat16 [4, 1024, 512], P('dp'), may hold values from -6 to 6
- segment_ids: int32 [4, 1024], P('dp'), may hold values from 0 to 7, never falling along the last dimension, each value on 1 to 256 neighbouring positions
- tile_live: int32 [4, 8, 8], P('dp'), may hold values 0 or 1
Outputs:
- grad_query: bfloat16 [4, 1024, 4096], P('dp', 'tsp', 'ctx')
- grad_keys: bfloat16 [4, 1024, 512], P('dp', ('ctx', 'tsp'))
- grad_values: bfloat16 [4, 1024, 512], P('dp', ('ctx', 'tsp'))
- grad_weight: float32 [4096, 8192], P('ctx', 'tsp')
Inputs may be any that keep to these rules, and one draw needn't show every extreme that they name: `segment_ids`: segment numbers never fall along a row and segment 0 is the source document; each segment has 1 to 256 tokens, one exactly that many.
All inputs are finite; a program needn't handle non-finite values. No bound on the sum of `tile_live` on one device may be relied on, other than what follows from the above.
Results may differ from a plain program's by a relative error of at most 0.0058.
Values may be sent and summed in bfloat16 or wider, within the bound.
A program may use at most 128 MiB of HBM per device.

v0:
```python
import math
import jax
import jax.numpy as jnp
from jax import lax
from jax.sharding import PartitionSpec as P

HEADS = 32
KV_HEADS = 4
HEAD_DIM = 128
TILE = 128


def merge_group(tensor_in):
    row_count = tensor_in.shape[0]
    folded = tensor_in.reshape(row_count, KV_HEADS, HEADS // KV_HEADS, HEAD_DIM).sum(axis=2)
    return folded.reshape(row_count, KV_HEADS * HEAD_DIM)


def per_device(grad_out, attn_out, out_weight, query, keys, values, segment_ids, tile_live):
    score_scale = 1.0 / math.sqrt(HEAD_DIM)
    out_all = attn_out[0]
    seq_len = out_all.shape[0]
    feat_width = out_all.shape[1]
    dy_block = lax.all_gather(grad_out, "ctx", axis=1, tiled=True)[0]
    proj_rows = lax.dot_general(
        dy_block, out_weight, (((1,), (1,)), ((), ())), preferred_element_type=jnp.float32
    )
    grad_part = proj_rows
    weight_part = lax.dot_general(
        out_all, dy_block, (((0,), (0,)), ((), ())), preferred_element_type=jnp.float32
    )
    grad_part, weight_part = (grad_part, weight_part)
    grad_weight = lax.psum(weight_part, "dp")
    out_grad = lax.psum_scatter(grad_part, "tsp", scatter_dimension=0, tiled=True).astype(
        jnp.bfloat16
    )
    quarter = out_grad.shape[0]
    row_start = lax.axis_index("tsp") * quarter
    heads_dev = feat_width // HEAD_DIM
    group_size = HEADS // KV_HEADS
    head_ids = lax.axis_index("ctx") * heads_dev + jnp.arange(heads_dev, dtype=jnp.int32)
    kv_ids = head_ids // group_size
    query_pos = row_start + jnp.arange(quarter, dtype=jnp.int32)
    key_pos = jnp.arange(seq_len, dtype=jnp.int32)
    tile_count = seq_len // TILE
    tile_rows = lax.dynamic_slice_in_dim(tile_live[0], row_start // TILE, quarter // TILE, 0)
    tile_mask = (
        jnp.broadcast_to(
            tile_rows[:, None, :, None], (quarter // TILE, TILE, tile_count, TILE)
        ).reshape(quarter, seq_len)
        == 1
    )
    same_tile = query_pos[:, None] // TILE == key_pos[None, :] // TILE
    segments = segment_ids[0]
    query_seg = lax.dynamic_slice_in_dim(segments, row_start, quarter, 0)
    same_doc = (segments[None, :] == query_seg[:, None]) | (segments[None, :] == 0)
    allowed = (tile_mask | same_tile) & same_doc & (key_pos[None, :] <= query_pos[:, None])

    def split_heads(tensor_in):
        return tensor_in.reshape(tensor_in.shape[0], heads_dev, HEAD_DIM).transpose(1, 0, 2)

    query_heads = split_heads(query[0])
    grad_heads = split_heads(out_grad)
    output_heads = split_heads(lax.dynamic_slice_in_dim(out_all, row_start, quarter, 0))
    key_table = keys[0].reshape(seq_len, KV_HEADS, HEAD_DIM)
    value_table = values[0].reshape(seq_len, KV_HEADS, HEAD_DIM)

    def one_head(head_items):
        query_head, grad_head, output_head, kv_index = head_items
        key_head = lax.dynamic_index_in_dim(key_table, kv_index, 1, keepdims=False)
        value_head = lax.dynamic_index_in_dim(value_table, kv_index, 1, keepdims=False)
        scores = (
            lax.dot_general(
                query_head, key_head, (((1,), (1,)), ((), ())), preferred_element_type=jnp.float32
            )
            * score_scale
        )
        scores = jnp.where(allowed, scores, -jnp.inf)
        row_max = jnp.max(scores, axis=1, keepdims=True)
        lse = row_max + jnp.log(jnp.sum(jnp.exp(scores - row_max), axis=1, keepdims=True))
        probs_f = jnp.where(allowed, jnp.exp(scores - lse), 0.0)
        probs = probs_f.astype(jnp.bfloat16)
        value_term = lax.dot_general(
            probs, grad_head, (((0,), (0,)), ((), ())), preferred_element_type=jnp.float32
        )
        dprobs = lax.dot_general(
            grad_head, value_head, (((1,), (1,)), ((), ())), preferred_element_type=jnp.float32
        )
        delta = jnp.sum(
            grad_head.astype(jnp.float32) * output_head.astype(jnp.float32), axis=1, keepdims=True
        )
        dscores = (probs_f * (dprobs - delta)).astype(jnp.bfloat16)
        query_grad = (
            jnp.dot(dscores, key_head, preferred_element_type=jnp.float32) * score_scale
        ).astype(jnp.bfloat16)
        key_term = (
            lax.dot_general(
                dscores, query_head, (((0,), (0,)), ((), ())), preferred_element_type=jnp.float32
            )
            * score_scale
        )
        return (query_grad, key_term, value_term)

    query_grads, key_terms, value_terms = lax.map(
        one_head, (query_heads, grad_heads, output_heads, kv_ids)
    )
    grad_query = query_grads.transpose(1, 0, 2).reshape(quarter, feat_width)
    key_cols = key_terms.transpose(1, 0, 2).reshape(seq_len, feat_width)
    value_cols = value_terms.transpose(1, 0, 2).reshape(seq_len, feat_width)
    key_recv, value_recv = (
        lax.all_to_all(key_cols, "ctx", split_axis=0, concat_axis=1, tiled=True),
        lax.all_to_all(value_cols, "ctx", split_axis=0, concat_axis=1, tiled=True),
    )
    key_part, value_part = (
        lax.psum_scatter(merge_group(key_recv), "tsp", scatter_dimension=0, tiled=True),
        lax.psum_scatter(merge_group(value_recv), "tsp", scatter_dimension=0, tiled=True),
    )
    grad_keys = key_part.astype(jnp.bfloat16)[None]
    grad_values = value_part.astype(jnp.bfloat16)[None]
    return (grad_query[None], grad_keys, grad_values, grad_weight)


def solution(mesh):
    placed = (
        P("dp", "ctx", "tsp"),
        P("dp", None, "ctx"),
        P("ctx", "tsp"),
        P("dp", "tsp", "ctx"),
        P("dp", None, None),
        P("dp", None, None),
        P("dp", None),
        P("dp", None, None),
    )
    return jax.shard_map(
        per_device,
        mesh=mesh,
        in_specs=placed,
        out_specs=(
            P("dp", "tsp", "ctx"),
            P("dp", ("ctx", "tsp"), None),
            P("dp", ("ctx", "tsp"), None),
            P("ctx", "tsp"),
        ),
        check_vma=False,
    )
```

profile of v0, /device:TPU:0, one launch (start us, length us, event | category | flops | bytes accessed | tf_op | source)
XLA Modules:
  0.0 900.4 jit_solution(15618256980744114519)
XLA Ops:
  8.0 154.0 %all-gather.2.cloned.1.call-done = bf16[1,1024,4096]{2,1,0:T(8,128)(2,1)} async-done(((bf16[1,256,4096]{2,1,0:T(8,128)(2,1)}), bf16[1,1024,4096]{2,1,0:T(8,128)(2,1)}) %all-gather.2.cloned.1.call-update) | async-done | bytes 8388624 | tf_op jit(solution)/shard_map/all_gather | solution.py:24
  161.9 15.1 %fusion.38 = f32[1024,1024]{1,0:T(8,128)} fusion(bf16[1024,4096]{1,0:T(8,128)(2,1)} %param.12, bf16[1,1024,4096]{2,1,0:T(8,128)(2,1)} %all-gather.2.cloned.1.call-done), kind=kOutput, calls=%fused_computation.47 | convolution fusion | flops 8589934592 | bytes 20971520 | tf_op jit(solution)/shard_map/dot_general | solution.py:25
  178.5 2.4 copy.46
  182.3 2.3 copy.49
  184.7 45.1 %reduce-scatter.4.cloned.1.call-done = f32[512,1024]{1,0:T(8,128)} async-done(((f32[1024,1024]{1,0:T(8,128)}), f32[512,1024]{1,0:T(8,128)}) %reduce-scatter.4.cloned.1.call-update) | async-done | bytes 2097168 | tf_op jit(solution)/shard_map/reduce_scatter | solution.py:34
  231.5 129.6 %while.15 = (s32[]{:T(128)}, bf16[8,512,128]{2,1,0:T(8,128)(2,1)}, f32[8,1024,128]{2,1,0:T(8,128)}, f32[8,1024,128]{2,1,0:T(8,128)}, bf16[8,512,128]{1,2,0:T(8,1...) while((s32[]{:T(128)}, bf16[8,512,128]{2,1,0:T(8,128)(2,1)}, ...), condition=%wide.region_5.6_spmd.clone, body=%wide.region_1.5_spmd.clone.sunk | while | flops 689437696 | bytes 16977196 | solution.py:104
  235.4 2.4 fusion.73
  238.3 2.7 multiply_convert_fusion.2
  243.1 2.4 fusion.77
  245.5 2.2 fusion.76
  251.6 2.4 fusion.73
  254.5 2.7 multiply_convert_fusion.2
  259.3 2.4 fusion.77
  261.8 2.2 fusion.76
  267.9 2.4 fusion.73
  270.8 2.7 multiply_convert_fusion.2
  275.6 2.4 fusion.77
  278.0 2.2 fusion.76
  284.1 2.4 fusion.73
  287.0 2.7 multiply_convert_fusion.2
  291.8 2.4 fusion.77
  300.3 2.4 fusion.73
  303.2 2.7 multiply_convert_fusion.2
  308.0 2.4 fusion.77
  316.5 2.4 fusion.73
  319.4 2.7 multiply_convert_fusion.2
  324.2 2.4 fusion.77
  332.7 2.4 fusion.73
  335.6 2.7 multiply_convert_fusion.2
  340.4 2.4 fusion.77
  348.9 2.4 fusion.73
  351.7 2.7 multiply_convert_fusion.2
  356.5 2.4 fusion.77
  361.1 6.6 copy.58
  367.7 4.9 all_to_all.27
  372.6 4.9 all-to-all-start.1
  377.5 6.5 copy.56
  384.0 4.9 all_to_all.24
  388.9 81.9 %all-to-all-done.1 = f32[4,256,1024]{2,1,0:T(8,128)} async-done(((f32[4,256,1024]{2,1,0:T(8,128)}), f32[4,256,1024]{2,1,0:T(8,128)}, u32[]{:S(2)}, u32[]{:S(2)}) %all-to-all-start.1) | async-done | bytes 4194336 | tf_op jit(solution)/shard_map/all_to_all | solution.py:112
  470.8 4.9 all-to-all-start
  475.8 5.1 copy.70
  480.9 3.2 reduce_sum.37
  485.2 83.3 %all-to-all-done = f32[4,256,1024]{2,1,0:T(8,128)} async-done(((f32[4,256,1024]{2,1,0:T(8,128)}), f32[4,256,1024]{2,1,0:T(8,128)}, u32[]{:S(2)}, u32[]{:S(2)}) %all-to-all-start) | async-done | bytes 4194336 | tf_op jit(solution)/shard_map/all_to_all | solution.py:111
  568.5 5.2 copy.69
  573.7 3.2 reduce_sum.36
  578.0 15.0 %fusion.36 = f32[1024,4096]{1,0:T(8,128)} fusion(bf16[1,1024,4096]{2,1,0:T(8,128)(2,1)} %all-gather.2.cloned.1.call-done, bf16[1,1024,1024]{2,1,0:T(8,128)(2,1)S(1)} %copy-done), kind=kOutput, calls=%fused_computation.45 | convolution fusion | flops 8589934592 | bytes 27262976 | tf_op jit(solution)/shard_map/dot_general | solution.py:29
  599.7 282.5 %all-reduce.2.cloned.1.call-done = f32[1024,4096]{1,0:T(8,128)} async-done(((f32[1024,4096]{1,0:T(8,128)}), f32[1024,4096]{1,0:T(8,128)}) %all-reduce.2.cloned.1.call-update) | async-done | bytes 16777232 | tf_op jit(solution)/shard_map/psum | solution.py:33
  882.2 11.7 %copy.104 = f32[1024,4096]{1,0:T(8,128)} copy(f32[1024,4096]{1,0:T(8,128)} %all-reduce.2.cloned.1.call-done) | data formatting | bytes 33554432
  (110 shorter events, 61.6 us)
Async XLA Ops:
  7.2 169.9 %copy-start = (bf16[1,1024,1024]{2,1,0:T(8,128)(2,1)S(1)}, bf16[1,1024,1024]{2,1,0:T(8,128)(2,1)}, u32[]{:S(2)}) copy-start(bf16[1,1024,1024]{2,1,0:T(8,128)(2,1)} %param.11) | copy-start | bytes 6291460
  7.2 154.7 %all-gather.2.cloned.1.call-start = ((), (), s32[]{:S(2)}) async-start(), calls=%async_computation.5 | async-start | bytes 10485760 | tf_op jit(solution)/shard_map/all_gather | solution.py:24
  7.9 221.8 %reduce-scatter.4.cloned.1.call-start = ((), (), s32[]{:S(2)}) async-start(), calls=%async_computation.6 | async-start | bytes 6291456 | tf_op jit(solution)/shard_map/reduce_scatter | solution.py:34
  178.5 2.4 copy-start.1
  180.9 3.6 copy-start.3
  180.9 3.7 copy-start.2
  372.6 98.3 %all-to-all-start.1 = ((f32[4,256,1024]{2,1,0:T(8,128)}), f32[4,256,1024]{2,1,0:T(8,128)}, u32[]{:S(2)}, u32[]{:S(2)}) async-start(f32[4,256,1024]{2,1,0:T(8,128)} %all_to_all.27), calls=%async_computation.3 | async-start | bytes 8388608 | tf_op jit(solution)/shard_map/all_to_all | solution.py:112
  470.8 97.7 %all-to-all-start = ((f32[4,256,1024]{2,1,0:T(8,128)}), f32[4,256,1024]{2,1,0:T(8,128)}, u32[]{:S(2)}, u32[]{:S(2)}) async-start(f32[4,256,1024]{2,1,0:T(8,128)} %all_to_all.24), calls=%async_computation.1 | async-start | bytes 8388608 | tf_op jit(solution)/shard_map/all_to_all | solution.py:111
  475.8 120.4 %reduce-scatter.8.cloned.1.call-start = ((), (), s32[]{:S(2)}) async-start(), calls=%async_computation.8 | async-start | bytes 786432 | tf_op jit(solution)/shard_map/reduce_scatter | solution.py:116
  485.1 112.8 %reduce-scatter.6.cloned.1.call-start = ((), (), s32[]{:S(2)}) async-start(), calls=%async_computation.7 | async-start | bytes 786432 | tf_op jit(solution)/shard_map/reduce_scatter | solution.py:115
  578.0 304.2 %all-reduce.2.cloned.1.call-start = ((), (), s32[]{:S(2)}) async-start(), calls=%async_computation.9 | async-start | bytes 33554432 | tf_op jit(solution)/shard_map/psum | solution.py:33
Sparse Core Ops, SparseCore 0:
  9.6 152.3 all-gather.1
  177.1 52.5 reduce-scatter.3
  485.3 15.0 reduce-scatter.7
  578.1 12.7 reduce-scatter.5
  593.8 288.3 all-reduce.1
where the time goes:
time: 902 us; the launch traced here: 900 us
  waiting for transfers between devices  648 us (72%)
  matrix products  124 us (14%)
  local copies, waits for them, and re-layouts  73.7 us (8%)
  loops' own time  15.8 us (2%)
  other arithmetic  15.5 us (2%)
  between operations  13.9 us (2%)
  starting transfers between devices  10.1 us (1%)
    psum x1, waiting for transfers between devices, per_device(): grad_weight = lax.psum(weight_part, 'dp')  282 us
    all_gather x1, waiting for transfers between devices, per_device(): dy_block = lax.all_gather(grad_out, 'ctx', axis=1, tiled=True)[0]  154 us
    all_to_all x1, waiting for transfers between devices, per_device(): lax.all_to_all(key_cols, 'ctx', split_axis=0, concat_axis=1, tiled=True)  83.3 us
    all_to_all x1, waiting for transfers between devices, per_device(): lax.all_to_all(value_cols, 'ctx', split_axis=0, concat_axis=1, tiled=True)  81.9 us
    reduce_scatter x1, waiting for transfers between devices, per_device(): lax.psum_scatter(grad_part, 'tsp', scatter_dimension=0, tiled=True)  45.1 us
    unnamed x17, local copies, waits for them, and re-layouts  31 us
    dot_general x8, matrix products, one_head(): lax.dot_general(grad_head, value_head, (((1,), (1,)), ((), ())), preferre...  21.9 us
    dot_general x8, matrix products, one_head(): lax.dot_general(probs, grad_head, (((0,), (0,)), ((), ())), preferred_ele...  19.1 us
  transfers between devices with their start and end apart: 7, of which 5 were waited for; matrix products, arithmetic and copies ran while one was open for 6% of the time, Pallas kernels for 0%

commit v1 on v0

--- a/solution.py
+++ b/solution.py
@@ -8,6 +8,22 @@
 KV_HEADS = 4
 HEAD_DIM = 128
 TILE = 128
+
+
+def ring_gather(x, axis, dim):
+    ways, here, turn = (lax.axis_size(axis), lax.axis_index(axis), x.shape[dim])
+    dims = [n * ways if d == dim else n for d, n in enumerate(x.shape)]
+    full = lax.dynamic_update_slice_in_dim(jnp.zeros(dims, x.dtype), x, here * turn, axis=dim)
+    going_up = going_down = x
+    for far in range(1, ways // 2 + 1):
+        going_up = lax.ppermute(going_up, axis, [(d, (d + 1) % ways) for d in range(ways)])
+        full = lax.dynamic_update_slice_in_dim(full, going_up, (here - far) % ways * turn, axis=dim)
+        if 2 * far < ways:
+            going_down = lax.ppermute(going_down, axis, [(d, (d - 1) % ways) for d in range(ways)])
+            full = lax.dynamic_update_slice_in_dim(
+                full, going_down, (here + far) % ways * turn, axis=dim
+            )
+    return full
 
 
 def merge_group(tensor_in):
@@ -21,7 +37,7 @@
     out_all = attn_out[0]
     seq_len = out_all.shape[0]
     feat_width = out_all.shape[1]
-    dy_block = lax.all_gather(grad_out, "ctx", axis=1, tiled=True)[0]
+    dy_block = ring_gather(grad_out, "ctx", 1)[0]
     proj_rows = lax.dot_general(
         dy_block, out_weight, (((1,), (1,)), ((), ())), preferred_element_type=jnp.float32
     )

time: 902 us -> 740 us (0.82)
  waiting for transfers between devices: 648 us -> 419 us
  other arithmetic: 15.5 us -> 37.1 us
  local copies, waits for them, and re-layouts: 73.7 us -> 95.3 us
  matrix products: 124 us -> 139 us
    psum x1, waiting for transfers between devices: 282 us -> 99.8 us  [per_device(): grad_weight = lax.psum(weight_part, 'dp')]
    all_gather x1 -> x0, waiting for transfers between devices: 154 us -> none  [per_device(): dy_block = lax.all_gather(grad_out, 'ctx', axis=1, tiled=True)[0]]
    ppermute x0 -> x3, waiting for transfers between devices: none -> 124 us  [the longest x2 89 us: ring_gather(): lax.ppermute(going_up, axis, [(d, (d + 1) % ways) for d in range(ways)])]
    all_to_all x1, waiting for transfers between devices: 83.3 us -> 66.5 us  [per_device(): lax.all_to_all(key_cols, 'ctx', split_axis=0, concat_axis=1, tiled=True)]
    reduce_sum x8, other arithmetic: 4.12 us -> 16.3 us  [one_head(): jnp.sum(jnp.exp(scores - row_max), axis=1, keepdims=True)]
    dynamic_update_slice x0 -> x4, local copies, waits for them, and re-layouts: none -> 10.9 us  [the longest x2 6.29 us: ring_gather(): lax.dynamic_update_slice_in_dim(full, going_up, (here - far) % ways * tur...]
    dot_general x8, matrix products: 18.9 us -> 29.4 us  [one_head(): lax.dot_general(query_head, key_head, (((1,), (1,)), ((), ())), preferred...]
    unnamed x17 -> x21, local copies, waits for them, and re-layouts: 31 us -> 36.9 us
  transfers between devices with their start and end apart: 7 -> 9, of which waited for: 5 -> 7; matrix products, arithmetic and copies ran while one was open for 6% -> 11% of each run, Pallas kernels for 0% -> 0%
where the time goes in v1:
time: 740 us; the launch traced here: 738 us
  waiting for transfers between devices  419 us (57%)
  matrix products  139 us (19%)
  local copies, waits for them, and re-layouts  95.3 us (13%)
  other arithmetic  37.1 us (5%)
  loops' own time  15.9 us (2%)
  starting transfers between devices  15.4 us (2%)
  between operations  15.3 us (2%)
    psum x1, waiting for transfers between devices, per_device(): grad_weight = lax.psum(weight_part, 'dp')  99.8 us
    ppermute x2, waiting for transfers between devices, ring_gather(): lax.ppermute(going_up, axis, [(d, (d + 1) % ways) for d in range(ways)])  89 us
    all_to_all x1, waiting for transfers between devices, per_device(): lax.all_to_all(value_cols, 'ctx', split_axis=0, concat_axis=1, tiled=True)  83 us
    all_to_all x1, waiting for transfers between devices, per_device(): lax.all_to_all(key_cols, 'ctx', split_axis=0, concat_axis=1, tiled=True)  66.5 us
    reduce_scatter x1, waiting for transfers between devices, per_device(): lax.psum_scatter(grad_part, 'tsp', scatter_dimension=0, tiled=True)  46.1 us
    unnamed x21, local copies, waits for them, and re-layouts  36.9 us
    ppermute x1, waiting for transfers between devices, ring_gather(): lax.ppermute(going_down, axis, [(d, (d - 1) % ways) for d in range(ways)])  34.8 us
    dot_general x8, matrix products, one_head(): lax.dot_general(query_head, key_head, (((1,), (1,)), ((), ())), preferred...  29.4 us
  transfers between devices with their start and end apart: 9, of which 7 were waited for; matrix products, arithmetic and copies ran while one was open for 11% of the time, Pallas kernels for 0%

profile of v1, /device:TPU:0, one launch (start us, length us, event | category | flops | bytes accessed | tf_op | source)
XLA Modules:
  0.0 737.5 jit_solution(16312091321168364071)
XLA Ops:
  8.1 3.1 collective-permute-start
  13.3 46.8 %collective-permute-done = bf16[1,256,4096]{2,1,0:T(8,128)(2,1)} collective-permute-done((bf16[1,256,4096]{2,1,0:T(8,128)(2,1)}, bf16[1,256,4096]{2,1,0:T(8,128)(2,1)}, u32[]{:S(2)}, u32[]{:S(2)}) %collective-permute-start) | collective-permute-done | bytes 2097184 | tf_op jit(solution)/shard_map/ppermute | solution.py:19
  60.0 4.3 squeeze.35
  65.8 3.2 bitcast_dynamic-update-slice_fusion.2
  69.0 34.8 %collective-permute-done.1 = bf16[1,256,4096]{2,1,0:T(8,128)(2,1)} collective-permute-done((bf16[1,256,4096]{2,1,0:T(8,128)(2,1)}, bf16[1,256,4096]{2,1,0:T(8,128)(2,1)}, u32[]{:S(2)}, u32[]{:S(2)}) %collective-permute-start.1) | collective-permute-done | bytes 2097184 | tf_op jit(solution)/shard_map/ppermute | solution.py:22
  103.7 3.1 bitcast_dynamic-update-slice_fusion.1
  106.9 42.2 %collective-permute-done.2 = bf16[1,256,4096]{2,1,0:T(8,128)(2,1)} collective-permute-done((bf16[1,256,4096]{2,1,0:T(8,128)(2,1)}, bf16[1,256,4096]{2,1,0:T(8,128)(2,1)}, u32[]{:S(2)}, u32[]{:S(2)}) %collective-permute-start.2) | collective-permute-done | bytes 2097184 | tf_op jit(solution)/shard_map/ppermute | solution.py:19
  149.1 3.1 bitcast_dynamic-update-slice_fusion
  152.2 15.1 %fusion.45 = f32[1024,1024]{1,0:T(8,128)} fusion(bf16[1024,4096]{1,0:T(8,128)(2,1)} %bitcast_dynamic-update-slice_fusion, bf16[1024,4096]{1,0:T(8,128)(2,1)} %param.12), kind=kOutput, calls=%fused_computation.81 | convolution fusion | flops 8589934592 | bytes 20971520 | tf_op jit(solution)/shard_map/dot_general | solution.py:41
  175.1 46.1 %reduce-scatter.4.cloned.1.call-done = f32[512,1024]{1,0:T(8,128)} async-done(((f32[1024,1024]{1,0:T(8,128)}), f32[512,1024]{1,0:T(8,128)}) %reduce-scatter.4.cloned.1.call-update) | async-done | bytes 2097168 | tf_op jit(solution)/shard_map/reduce_scatter | solution.py:50
  221.1 2.7 bitcast_bitcast_fusion
  223.8 165.9 %while.15 = (s32[]{:T(128)}, bf16[8,512,128]{2,1,0:T(8,128)(2,1)}, f32[8,1024,128]{2,1,0:T(8,128)}, f32[8,1024,128]{2,1,0:T(8,128)}, bf16[8,512,128]{1,2,0:T(8,1...) while((s32[]{:T(128)}, bf16[8,512,128]{2,1,0:T(8,128)(2,1)}, ...), condition=%wide.region_5.6_spmd.clone, body=%wide.region_1.5_spmd.clone.sunk | while | flops 689437696 | bytes 25365832 | solution.py:120
  226.6 3.7 fusion.72
  234.6 2.5 multiply_convert_fusion.2
  241.3 3.2 fusion.76
  247.3 3.7 fusion.72
  255.3 2.5 multiply_convert_fusion.2
  262.0 3.3 fusion.76
  268.0 3.7 fusion.72
  276.0 2.5 multiply_convert_fusion.2
  282.8 3.3 fusion.76
  288.8 3.7 fusion.72
  303.5 3.3 fusion.76
  309.5 3.7 fusion.72
  317.5 2.5 multiply_convert_fusion.2
  324.2 3.3 fusion.76
  330.2 3.7 fusion.72
  345.0 3.3 fusion.76
  351.0 3.7 fusion.72
  359.0 2.5 multiply_convert_fusion.2
  365.7 3.2 fusion.76
  371.7 3.7 fusion.72
  386.4 3.3 fusion.76
  389.7 6.6 copy.60
  396.3 4.9 all_to_all.24
  401.2 4.9 all-to-all-start
  406.1 14.7 %convolution_bitcast_fusion.1 = f32[1024,4096]{0,1:T(8,128)} fusion(bf16[1024,4096]{1,0:T(8,128)(2,1)} %bitcast_dynamic-update-slice_fusion, bf16[1,1024,1024]{2,1,0:T(8,128)(2,1)S(1)} %copy-done), kind=kOutput, calls=%fused_computation.45 | convolution fusion | flops 8589934592 | bytes 27262976 | tf_op jit(solution)/shard_map/dot_general | solution.py:45
  420.9 7.0 copy.62
  427.9 4.9 all_to_all.27
  432.8 66.5 %all-to-all-done = f32[4,256,1024]{2,1,0:T(8,128)} async-done(((f32[4,256,1024]{2,1,0:T(8,128)}), f32[4,256,1024]{2,1,0:T(8,128)}, u32[]{:S(2)}, u32[]{:S(2)}) %all-to-all-start) | async-done | bytes 4194336 | tf_op jit(solution)/shard_map/all_to_all | solution.py:127
  499.3 4.9 all-to-all-start.1
  504.6 5.1 copy.74
  509.7 3.2 reduce_sum.36
  514.0 83.0 %all-to-all-done.1 = f32[4,256,1024]{2,1,0:T(8,128)} async-done(((f32[4,256,1024]{2,1,0:T(8,128)}), f32[4,256,1024]{2,1,0:T(8,128)}, u32[]{:S(2)}, u32[]{:S(2)}) %all-to-all-start.1) | async-done | bytes 4194336 | tf_op jit(solution)/shard_map/all_to_all | solution.py:128
  597.0 5.2 copy.75
  602.2 3.2 reduce_sum.37
  609.7 99.8 %all-reduce.2.cloned.1.call-done = f32[1024,4096]{0,1:T(8,128)} async-done(((f32[1024,4096]{0,1:T(8,128)}), f32[1024,4096]{0,1:T(8,128)}) %all-reduce.2.cloned.1.call-update) | async-done | bytes 16777232 | tf_op jit(solution)/shard_map/psum | solution.py:49
  709.5 17.4 %copy.66 = f32[1024,4096]{1,0:T(8,128)} copy(f32[1024,4096]{0,1:T(8,128)} %all-reduce.2.cloned.1.call-done) | data formatting | bytes 33554432
  (138 shorter events, 102.3 us)
Async XLA Ops:
  8.0 165.5 %copy-start = (bf16[1,1024,1024]{2,1,0:T(8,128)(2,1)S(1)}, bf16[1,1024,1024]{2,1,0:T(8,128)(2,1)}, u32[]{:S(2)}) copy-start(bf16[1,1024,1024]{2,1,0:T(8,128)(2,1)} %param.11) | copy-start | bytes 6291460
  8.0 213.1 %reduce-scatter.4.cloned.1.call-start = ((), (), s32[]{:S(2)}) async-start(), calls=%async_computation.5 | async-start | bytes 6291456 | tf_op jit(solution)/shard_map/reduce_scatter | solution.py:50
  8.1 52.0 %collective-permute-start = (bf16[1,256,4096]{2,1,0:T(8,128)(2,1)}, bf16[1,256,4096]{2,1,0:T(8,128)(2,1)}, u32[]{:S(2)}, u32[]{:S(2)}) collective-permute-start(bf16[1,256,4096]{2,1,0:T(8,128)(2,1)} %param.10), channel_id=1, source_target_pairs={{0,2},{2,4},{4,6},{6,0},{1,3},{3,5},{5,7},{7,1},{8,10},{10,12},{12... | collective-permute-start | bytes 6291464 | tf_op jit(solution)/shard_map/ppermute | solution.py:19
  11.2 92.6 %collective-permute-start.1 = (bf16[1,256,4096]{2,1,0:T(8,128)(2,1)}, bf16[1,256,4096]{2,1,0:T(8,128)(2,1)}, u32[]{:S(2)}, u32[]{:S(2)}) collective-permute-start(bf16[1,256,4096]{2,1,0:T(8,128)(2,1)} %param.10), channel_id=1, source_target_pairs={{0,6},{2,0},{4,2},{6,4},{1,7},{3,1},{5,3},{7,5},{8,14},{10,8},{12,... | collective-permute-start | bytes 6291464 | tf_op jit(solution)/shard_map/ppermute | solution.py:22
  13.3 51.1 %copy-start.2 = (bf16[1,256,4096]{2,1,0:T(8,128)(2,1)S(1)}, bf16[1,256,4096]{2,1,0:T(8,128)(2,1)}, u32[]{:S(2)}) copy-start(bf16[1,256,4096]{2,1,0:T(8,128)(2,1)} %param.10) | copy-start | bytes 6291460
  60.0 89.0 %collective-permute-start.2 = (bf16[1,256,4096]{2,1,0:T(8,128)(2,1)}, bf16[1,256,4096]{2,1,0:T(8,128)(2,1)}, u32[]{:S(2)}, u32[]{:S(2)}) collective-permute-start(bf16[1,256,4096]{2,1,0:T(8,128)(2,1)} %collective-permute-done), channel_id=1, source_target_pairs={{0,2},{2,4},{4,6},{6,0},{1,3},{3,5},{5,7},{7,1},{8,10},{10,12},{12... | collective-permute-start | bytes 6291464 | tf_op jit(solution)/shard_map/ppermute | solution.py:19
  167.3 1.2 copy-start.3
  169.8 2.4 copy-start.4
  173.5 1.4 copy-start.6
  173.5 1.5 copy-start.5
  231.3 3.3 copy-start.1
  252.0 3.3 copy-start.1
  272.8 3.3 copy-start.1
  293.5 3.3 copy-start.1
  314.2 3.3 copy-start.1
  335.0 3.3 copy-start.1
  355.7 3.3 copy-start.1
  376.4 3.3 copy-start.1
  401.2 98.2 %all-to-all-start = ((f32[4,256,1024]{2,1,0:T(8,128)}), f32[4,256,1024]{2,1,0:T(8,128)}, u32[]{:S(2)}, u32[]{:S(2)}) async-start(f32[4,256,1024]{2,1,0:T(8,128)} %all_to_all.24), calls=%async_computation.1 | async-start | bytes 8388608 | tf_op jit(solution)/shard_map/all_to_all | solution.py:127
  406.0 303.4 %all-reduce.2.cloned.1.call-start = ((), (), s32[]{:S(2)}) async-start(), calls=%async_computation.8 | async-start | bytes 33554432 | tf_op jit(solution)/shard_map/psum | solution.py:49
  499.3 97.7 %all-to-all-start.1 = ((f32[4,256,1024]{2,1,0:T(8,128)}), f32[4,256,1024]{2,1,0:T(8,128)}, u32[]{:S(2)}, u32[]{:S(2)}) async-start(f32[4,256,1024]{2,1,0:T(8,128)} %all_to_all.27), calls=%async_computation.3 | async-start | bytes 8388608 | tf_op jit(solution)/shard_map/all_to_all | solution.py:128
  504.3 222.6 %reduce-scatter.6.cloned.1.call-start = ((), (), s32[]{:S(2)}) async-start(), calls=%async_computation.6 | async-start | bytes 786432 | tf_op jit(solution)/shard_map/reduce_scatter | solution.py:131
  514.0 214.7 %reduce-scatter.8.cloned.1.call-start = ((), (), s32[]{:S(2)}) async-start(), calls=%async_computation.7 | async-start | bytes 786432 | tf_op jit(solution)/shard_map/reduce_scatter | solution.py:132
Sparse Core Ops, SparseCore 0:
  167.4 53.6 reduce-scatter.3
  514.1 14.7 reduce-scatter.5
  606.6 12.7 reduce-scatter.7
Sparse Core Ops, SparseCore 1:
  420.9 288.5 all-reduce.1
